TPU v7x, 512 devices: a whole 4x8x8 slice. The times are simulated.
512 devices in a mesh: pipe: 4 (over x), tx: 4 (over y_lo, core), ty: 32 (over z, y_hi).
Axes of the slice: x: 4, y: 8 (y_hi: 4, y_lo: 2; y = y_hi * 2 + y_lo), z: 8, core: 2. Of those that a mesh axis runs over, the one named last changes fastest.
Arguments:
- stored: bfloat16 [4, 2, 4, 32, 256, 512], P('pipe', None, 'tx', 'ty'), may hold values from -6 to 6
- cotangent: bfloat16 [2, 4, 32, 256, 512], P(None, 'tx', 'ty'), may hold values from -6 to 6
- weight: bfloat16 [4, 512, 512], P('pipe'), may hold values from -0.25 to 0.25
- local_edges: bfloat16 [2, 4, 32, 2, 2, 128, 128], P(None, 'tx', 'ty'), may hold values from -0.21875 to 0.21875
- halo_edges: bfloat16 [2, 4, 32, 4, 2, 128, 128], P(None, 'tx', 'ty'), may hold values from -0.21875 to 0.21875
- pattern: int32 [2, 4, 32, 2, 6], P(None, 'tx', 'ty'), may hold values 0 or 1
- pick: int32 [2, 4, 32, 4], P(None, 'tx', 'ty'), may hold values from 0 to 1
Outputs:
- grad_weight: float32 [4, 512, 512], P('pipe', ('tx', 'ty'))
- grad_input: bfloat16 [4, 2, 4, 32, 256, 512], P('pipe', None, 'tx', 'ty')
Inputs may be any that keep to these rules, and one draw needn't show every extreme that they name: `pattern`: 1 where a block of edges is present, 0 where it is absent. `pick`: a block index of the sending tile.
All inputs are finite; a program needn't handle non-finite values.
Results may differ from a plain program's by a relative error of at most 0.015.
Values may be sent and summed in bfloat16 or wider, within the bound.
A program may use at most 64 MiB of HBM per device.

v0:
```python
import math

import jax
import jax.numpy as jnp
from jax import lax
from jax.sharding import PartitionSpec as P


def shifted(value, axis, steps):
    count = lax.axis_size(axis)
    leading, last = (max(0, -steps), min(count, count - steps))
    return lax.ppermute(value, axis, [(source, source + steps) for source in range(leading, last)])


def silu_slope(value):
    sigma = jax.nn.sigmoid(value)
    return sigma * (1.0 + value * (1.0 - sigma))


def take_entry(array, index):
    return lax.dynamic_index_in_dim(array, index, 0, keepdims=False)


def per_device(stored, cotangent, weight, local_edges, halo_edges, pattern, pick):
    sections = lax.axis_size("pipe")
    section = lax.axis_index("pipe")
    stashed = stored[0, :, 0, 0]
    given = cotangent[:, 0, 0]
    matrix = weight[0]
    batches, nodes, width = stashed.shape
    blocks = local_edges.shape[3]
    block_size = local_edges.shape[5]
    block_mask = pattern[:, 0, 0].astype(jnp.bfloat16)
    local_masked = local_edges[:, 0, 0] * block_mask[:, :, :blocks, None, None]
    halo_masked = (
        halo_edges[:, 0, 0] * jnp.swapaxes(block_mask[:, :, blocks:], 1, 2)[:, :, :, None, None]
    )
    placing = (
        pick[:, 0, 0][:, :, None] == jnp.arange(blocks, dtype=jnp.int32)[None, None, :]
    ).astype(jnp.float32)
    carried = jnp.zeros((nodes, width), jnp.bfloat16)
    results = jnp.zeros((batches, nodes, width), jnp.bfloat16)
    weight_total = jnp.zeros((width, width), jnp.float32)
    rounds = sections + batches - 1
    for step in range(rounds):
        offset_batch = step - (sections - 1 - section)
        active = (offset_batch >= 0) & (offset_batch < batches)
        batch = jnp.clip(offset_batch, 0, batches - 1)
        upstream = jnp.where(section == sections - 1, take_entry(given, batch), carried)
        features = take_entry(stashed, batch)
        pre_activation = jnp.dot(features, matrix, preferred_element_type=jnp.float32)
        slope_grad = (upstream.astype(jnp.float32) * silu_slope(pre_activation)).astype(
            jnp.bfloat16
        )
        message_grad = lax.dot_general(
            slope_grad, matrix, (((1,), (1,)), ((), ())), preferred_element_type=jnp.float32
        ).astype(jnp.bfloat16)
        grad_blocks = message_grad.reshape(blocks, block_size, width)
        inner = jnp.einsum(
            "bcij,bik->cjk",
            take_entry(local_masked, batch),
            grad_blocks,
            preferred_element_type=jnp.float32,
        )
        outward = jnp.einsum(
            "ebij,bik->ejk",
            take_entry(halo_masked, batch),
            grad_blocks,
            preferred_element_type=jnp.float32,
        ).astype(jnp.bfloat16)
        arrived = jnp.stack(
            [
                shifted(outward[0], "tx", -1),
                shifted(outward[1], "tx", 1),
                shifted(outward[2], "ty", -1),
                shifted(outward[3], "ty", 1),
            ]
        ).astype(jnp.float32)
        placed = jnp.einsum(
            "ec,ejk->cjk", take_entry(placing, batch), arrived, precision=lax.Precision.HIGHEST
        )
        total = upstream.astype(jnp.float32) + (inner + placed).reshape(nodes, width)
        features, slope_grad, result = (features, slope_grad, total.astype(jnp.bfloat16))
        results = jnp.where(
            active, lax.dynamic_update_index_in_dim(results, result, batch, 0), results
        )
        product = lax.dot_general(
            features, slope_grad, (((0,), (0,)), ((), ())), preferred_element_type=jnp.float32
        )
        weight_total = weight_total + jnp.where(active, product, 0.0)
        if step + 1 < rounds:
            carried = shifted(result, "pipe", -1)
    scale = 1.0 / math.sqrt(batches * nodes * lax.axis_size("tx") * lax.axis_size("ty"))
    summed = lax.psum_scatter(weight_total, ("tx", "ty"), scatter_dimension=0, tiled=True)
    return ((summed * scale)[None], results[None, :, None, None])


def solution(mesh):
    in_specs = (
        P("pipe", None, "tx", "ty", None, None),
        P(None, "tx", "ty", None, None),
        P("pipe", None, None),
        P(None, "tx", "ty", None, None, None, None),
        P(None, "tx", "ty", None, None, None, None),
        P(None, "tx", "ty", None, None),
        P(None, "tx", "ty", None),
    )
    out_specs = (P("pipe", ("tx", "ty"), None), P("pipe", None, "tx", "ty", None, None))
    return jax.shard_map(
        per_device, mesh=mesh, in_specs=in_specs, out_specs=out_specs, check_vma=False
    )
```

profile of v0, /device:TPU:1, one launch (start us, length us, event | category | flops | bytes accessed | tf_op | source)
XLA Modules:
  0.0 365.4 jit_solution(13734712674702636249)
XLA Ops:
  7.2 1.0 copy-done
  8.2 1.6 fusion.24
  9.9 0.3 convolution_convert_fusion.4
  11.5 0.7 slice_bitcast_fusion.19
  12.1 8.8 %collective-permute-start = (bf16[128,512]{1,0:T(8,128)(2,1)}, bf16[128,512]{1,0:T(8,128)(2,1)S(1)}, u32[]{:S(2)}, u32[]{:S(2)}) collective-permute-start(bf16[128,512]{1,0:T(8,128)(2,1)} %get-tuple-element.22), channel_id=1, source_target_pairs={{32,0},{64,32},{96,64},{33,1},{65,33},{97,65},{34,2},{66,34},{98,6... | collective-permute-start | bytes 393224 | tf_op jit(solution)/shard_map/ppermute | solution.py:12
  20.9 1.9 collective-permute-start.1
  22.9 1.3 collective-permute-start.2
  24.2 5.5 %collective-permute-start.3 = (bf16[128,512]{1,0:T(8,128)(2,1)S(1)}, bf16[128,512]{1,0:T(8,128)(2,1)}, u32[]{:S(2)}, u32[]{:S(2)}) collective-permute-start(bf16[128,512]{1,0:T(8,128)(2,1)S(1)} %get-tuple-element.23), channel_id=1, source_target_pairs={{0,1},{1,2},{2,3},{3,4},{4,5},{5,6},{6,7},{7,8},{8,9},{9,10},{10,1... | collective-permute-start | bytes 393224 | tf_op jit(solution)/shard_map/ppermute | solution.py:12
  29.8 0.8 constant_dynamic-slice_fusion
  30.6 0.8 copy.37
  31.4 0.7 copy-done.16
  32.1 0.6 collective-permute-done.3
  32.7 1.0 pad_maximum_fusion
  33.7 0.6 fusion.61
  34.8 0.8 copy-done.2
  35.7 1.3 collective-permute-start.4
  37.0 0.8 copy.43
  37.8 6.3 %collective-permute-done.4 = bf16[256,512]{1,0:T(8,128)(2,1)} collective-permute-done((bf16[256,512]{1,0:T(8,128)(2,1)S(1)}, bf16[256,512]{1,0:T(8,128)(2,1)}, u32[]{:S(2)}, u32[]{:S(2)}) %collective-permute-start.4) | collective-permute-done | bytes 262176 | tf_op jit(solution)/shard_map/ppermute | solution.py:12
  44.1 1.4 fusion.16
  45.5 0.3 convolution_convert_fusion.3
  46.2 4.2 %collective-permute-start.5 = (bf16[128,512]{1,0:T(8,128)(2,1)S(1)}, bf16[128,512]{1,0:T(8,128)(2,1)S(1)}, u32[]{:S(2)}, u32[]{:S(2)}) collective-permute-start(bf16[128,512]{1,0:T(8,128)(2,1)S(1)} %get-tuple-element.18), channel_id=1, source_target_pairs={{32,0},{64,32},{96,64},{33,1},{65,33},{97,65},{34,2},{66,34},{98,6... | collective-permute-start | bytes 393224 | tf_op jit(solution)/shard_map/ppermute | solution.py:12
  50.5 1.9 collective-permute-start.6
  52.4 1.3 collective-permute-start.7
  53.7 5.9 %collective-permute-start.8 = (bf16[128,512]{1,0:T(8,128)(2,1)S(1)}, bf16[128,512]{1,0:T(8,128)(2,1)S(1)}, u32[]{:S(2)}, u32[]{:S(2)}) collective-permute-start(bf16[128,512]{1,0:T(8,128)(2,1)S(1)} %get-tuple-element.19), channel_id=1, source_target_pairs={{0,1},{1,2},{2,3},{3,4},{4,5},{5,6},{6,7},{7,8},{8,9},{9,10},{10,1... | collective-permute-start | bytes 393224 | tf_op jit(solution)/shard_map/ppermute | solution.py:12
  59.7 2.9 collective-permute-done.7
  62.7 0.6 fusion.59
  63.9 1.9 fusion.72
  65.7 1.3 collective-permute-start.9
  67.2 0.8 copy-done.5
  68.2 1.3 dynamic-slice.20
  70.2 3.5 collective-permute-done.9
  73.6 1.4 fusion.18
  75.8 5.1 %collective-permute-start.10 = (bf16[128,512]{1,0:T(8,128)(2,1)S(1)}, bf16[128,512]{1,0:T(8,128)(2,1)S(1)}, u32[]{:S(2)}, u32[]{:S(2)}) collective-permute-start(bf16[128,512]{1,0:T(8,128)(2,1)S(1)} %get-tuple-element.14), channel_id=1, source_target_pairs={{32,0},{64,32},{96,64},{33,1},{65,33},{97,65},{34,2},{66,34},{98,6... | collective-permute-start | bytes 393224 | tf_op jit(solution)/shard_map/ppermute | solution.py:12
  80.8 1.9 collective-permute-start.11
  82.8 1.3 collective-permute-start.12
  84.1 6.4 %collective-permute-start.13 = (bf16[128,512]{1,0:T(8,128)(2,1)S(1)}, bf16[128,512]{1,0:T(8,128)(2,1)S(1)}, u32[]{:S(2)}, u32[]{:S(2)}) collective-permute-start(bf16[128,512]{1,0:T(8,128)(2,1)S(1)} %get-tuple-element.15), channel_id=1, source_target_pairs={{0,1},{1,2},{2,3},{3,4},{4,5},{5,6},{6,7},{7,8},{8,9},{9,10},{10,1... | collective-permute-start | bytes 393224 | tf_op jit(solution)/shard_map/ppermute | solution.py:12
  90.4 0.3 convolution_select_fusion.4
  90.8 3.5 collective-permute-done.12
  94.3 0.6 fusion.57
  95.2 1.1 fusion.71
  96.3 1.3 collective-permute-start.14
  98.0 7.7 %collective-permute-done.14 = bf16[256,512]{1,0:T(8,128)(2,1)S(1)} collective-permute-done((bf16[256,512]{1,0:T(8,128)(2,1)S(1)}, bf16[256,512]{1,0:T(8,128)(2,1)S(1)}, u32[]{:S(2)}, u32[]{:S(2)}) %collective-permute-start.14) | collective-permute-done | bytes 262176 | tf_op jit(solution)/shard_map/ppermute | solution.py:12
  105.7 0.4 fusion.20
  106.1 0.3 convolution_convert_fusion.1
  106.8 3.2 collective-permute-start.15
  110.0 2.4 collective-permute-start.16
  112.4 1.3 collective-permute-start.17
  113.7 6.7 %collective-permute-start.18 = (bf16[128,512]{1,0:T(8,128)(2,1)S(1)}, bf16[128,512]{1,0:T(8,128)(2,1)S(1)}, u32[]{:S(2)}, u32[]{:S(2)}) collective-permute-start(bf16[128,512]{1,0:T(8,128)(2,1)S(1)} %get-tuple-element.11), channel_id=1, source_target_pairs={{0,1},{1,2},{2,3},{3,4},{4,5},{5,6},{6,7},{7,8},{8,9},{9,10},{10,1... | collective-permute-start | bytes 393224 | tf_op jit(solution)/shard_map/ppermute | solution.py:12
  120.4 0.3 fusion.2
  120.8 3.0 collective-permute-done.17
  123.9 0.6 fusion.55
  124.9 1.3 collective-permute-start.19
  126.6 7.6 %collective-permute-done.19 = bf16[256,512]{1,0:T(8,128)(2,1)S(1)} collective-permute-done((bf16[256,512]{1,0:T(8,128)(2,1)S(1)}, bf16[256,512]{1,0:T(8,128)(2,1)S(1)}, u32[]{:S(2)}, u32[]{:S(2)}) %collective-permute-start.19) | collective-permute-done | bytes 262176 | tf_op jit(solution)/shard_map/ppermute | solution.py:12
  134.1 0.4 fusion.22
  135.6 3.3 collective-permute-start.20
  138.9 2.3 collective-permute-start.21
  141.1 1.3 collective-permute-start.22
  142.4 6.9 %collective-permute-start.23 = (bf16[128,512]{1,0:T(8,128)(2,1)S(1)}, bf16[128,512]{1,0:T(8,128)(2,1)S(1)}, u32[]{:S(2)}, u32[]{:S(2)}) collective-permute-start(bf16[128,512]{1,0:T(8,128)(2,1)S(1)} %get-tuple-element.7), channel_id=1, source_target_pairs={{0,1},{1,2},{2,3},{3,4},{4,5},{5,6},{6,7},{7,8},{8,9},{9,10},{10,1... | collective-permute-start | bytes 393224 | tf_op jit(solution)/shard_map/ppermute | solution.py:12
  149.4 1.3 fusion
  150.8 2.0 collective-permute-done.22
  152.8 0.6 fusion.53
  153.7 0.7 copy-done.13
  154.6 202.7 %all-reduce.3.cloned.1.call-done = f32[512,512]{1,0:T(8,128)} async-done(((f32[512,512]{1,0:T(8,128)}), f32[512,512]{1,0:T(8,128)}) %all-reduce.3.cloned.1.call-update) | async-done | bytes 1048592
  357.3 1.3 fusion.118
  (83 shorter events, 7.5 us)
Async XLA Ops:
  7.2 1.0 copy-start
  7.2 350.1 %all-reduce.3.cloned.1.call-start = ((), (), s32[]{:S(2)}) async-start(), calls=%async_computation | async-start | bytes 2097152
  8.2 1.6 copy-start.1
  9.8 0.7 copy-start.3
  9.8 0.7 copy-start.15
  9.9 1.1 copy-start.8
  11.4 18.3 %copy-start.14 = (bf16[2,1,1,2,2,128,128]{6,5,4,3,2,1,0:T(8,128)(2,1)S(1)}, bf16[2,1,1,2,2,128,128]{6,5,4,3,2,1,0:T(8,128)(2,1)}, u32[]{:S(2)}) copy-start(bf16[2,1,1,2,2,128,128]{6,5,4,3,2,1,0:T(8,128)(2,1)} %param.10) | copy-start | bytes 786436
  12.1 20.0 %collective-permute-start = (bf16[128,512]{1,0:T(8,128)(2,1)}, bf16[128,512]{1,0:T(8,128)(2,1)S(1)}, u32[]{:S(2)}, u32[]{:S(2)}) collective-permute-start(bf16[128,512]{1,0:T(8,128)(2,1)} %get-tuple-element.22), channel_id=1, source_target_pairs={{32,0},{64,32},{96,64},{33,1},{65,33},{97,65},{34,2},{66,34},{98,6... | collective-permute-start | bytes 393224 | tf_op jit(solution)/shard_map/ppermute | solution.py:12
  20.9 11.2 %collective-permute-start.1 = (bf16[128,512]{1,0:T(8,128)(2,1)S(1)}, bf16[128,512]{1,0:T(8,128)(2,1)S(1)}, u32[]{:S(2)}, u32[]{:S(2)}) collective-permute-start(bf16[128,512]{1,0:T(8,128)(2,1)S(1)} %get-tuple-element.25), channel_id=1, source_target_pairs={{0,32},{32,64},{64,96},{1,33},{33,65},{65,97},{2,34},{34,66},{66,9... | collective-permute-start | bytes 393224 | tf_op jit(solution)/shard_map/ppermute | solution.py:12
  22.9 9.3 %collective-permute-start.2 = (bf16[128,512]{1,0:T(8,128)(2,1)S(1)}, bf16[128,512]{1,0:T(8,128)(2,1)S(1)}, u32[]{:S(2)}, u32[]{:S(2)}) collective-permute-start(bf16[128,512]{1,0:T(8,128)(2,1)S(1)} %get-tuple-element.24), channel_id=1, source_target_pairs={{1,0},{2,1},{3,2},{4,3},{5,4},{6,5},{7,6},{8,7},{9,8},{10,9},{11,1... | collective-permute-start | bytes 393224 | tf_op jit(solution)/shard_map/ppermute | solution.py:12
  24.2 8.5 %collective-permute-start.3 = (bf16[128,512]{1,0:T(8,128)(2,1)S(1)}, bf16[128,512]{1,0:T(8,128)(2,1)}, u32[]{:S(2)}, u32[]{:S(2)}) collective-permute-start(bf16[128,512]{1,0:T(8,128)(2,1)S(1)} %get-tuple-element.23), channel_id=1, source_target_pairs={{0,1},{1,2},{2,3},{3,4},{4,5},{5,6},{6,7},{7,8},{8,9},{9,10},{10,1... | collective-permute-start | bytes 393224 | tf_op jit(solution)/shard_map/ppermute | solution.py:12
  31.4 0.7 copy-start.16
  33.7 0.9 copy-start.11
  34.6 1.0 copy-start.2
  35.6 1.4 copy-start.7
  35.7 8.4 %collective-permute-start.4 = (bf16[256,512]{1,0:T(8,128)(2,1)S(1)}, bf16[256,512]{1,0:T(8,128)(2,1)}, u32[]{:S(2)}, u32[]{:S(2)}) collective-permute-start(bf16[256,512]{1,0:T(8,128)(2,1)S(1)} %fusion.25), channel_id=1, source_target_pairs={{128,0},{256,128},{384,256},{129,1},{257,129},{385,257},{130,2},{2... | collective-permute-start | bytes 786440 | tf_op jit(solution)/shard_map/ppermute | solution.py:12
  46.2 13.5 %collective-permute-start.5 = (bf16[128,512]{1,0:T(8,128)(2,1)S(1)}, bf16[128,512]{1,0:T(8,128)(2,1)S(1)}, u32[]{:S(2)}, u32[]{:S(2)}) collective-permute-start(bf16[128,512]{1,0:T(8,128)(2,1)S(1)} %get-tuple-element.18), channel_id=1, source_target_pairs={{32,0},{64,32},{96,64},{33,1},{65,33},{97,65},{34,2},{66,34},{98,6... | collective-permute-start | bytes 393224 | tf_op jit(solution)/shard_map/ppermute | solution.py:12
  50.5 9.3 %collective-permute-start.6 = (bf16[128,512]{1,0:T(8,128)(2,1)S(1)}, bf16[128,512]{1,0:T(8,128)(2,1)S(1)}, u32[]{:S(2)}, u32[]{:S(2)}) collective-permute-start(bf16[128,512]{1,0:T(8,128)(2,1)S(1)} %get-tuple-element.21), channel_id=1, source_target_pairs={{0,32},{32,64},{64,96},{1,33},{33,65},{65,97},{2,34},{34,66},{66,9... | collective-permute-start | bytes 393224 | tf_op jit(solution)/shard_map/ppermute | solution.py:12
  52.4 10.2 %collective-permute-start.7 = (bf16[128,512]{1,0:T(8,128)(2,1)S(1)}, bf16[128,512]{1,0:T(8,128)(2,1)S(1)}, u32[]{:S(2)}, u32[]{:S(2)}) collective-permute-start(bf16[128,512]{1,0:T(8,128)(2,1)S(1)} %get-tuple-element.20), channel_id=1, source_target_pairs={{1,0},{2,1},{3,2},{4,3},{5,4},{6,5},{7,6},{8,7},{9,8},{10,9},{11,1... | collective-permute-start | bytes 393224 | tf_op jit(solution)/shard_map/ppermute | solution.py:12
  53.7 8.9 %collective-permute-start.8 = (bf16[128,512]{1,0:T(8,128)(2,1)S(1)}, bf16[128,512]{1,0:T(8,128)(2,1)S(1)}, u32[]{:S(2)}, u32[]{:S(2)}) collective-permute-start(bf16[128,512]{1,0:T(8,128)(2,1)S(1)} %get-tuple-element.19), channel_id=1, source_target_pairs={{0,1},{1,2},{2,3},{3,4},{4,5},{5,6},{6,7},{7,8},{8,9},{9,10},{10,1... | collective-permute-start | bytes 393224 | tf_op jit(solution)/shard_map/ppermute | solution.py:12
  62.7 0.9 copy-start.10
  63.8 3.2 copy-start.6
  65.7 7.9 %collective-permute-start.9 = (bf16[256,512]{1,0:T(8,128)(2,1)}, bf16[256,512]{1,0:T(8,128)(2,1)}, u32[]{:S(2)}, u32[]{:S(2)}) collective-permute-start(bf16[256,512]{1,0:T(8,128)(2,1)} %get-tuple-element.32), channel_id=1, source_target_pairs={{128,0},{256,128},{384,256},{129,1},{257,129},{385,257},{130,2},{2... | collective-permute-start | bytes 786440 | tf_op jit(solution)/shard_map/ppermute | solution.py:12
  67.0 0.9 copy-start.5
  75.7 14.7 %copy-start.4 = (bf16[256,512]{1,0:T(8,128)(2,1)S(1)}, bf16[256,512]{1,0:T(8,128)(2,1)}, u32[]{:S(2)}) copy-start(bf16[256,512]{1,0:T(8,128)(2,1)} %copy-done.3) | copy-start | bytes 786436
  75.8 15.0 %collective-permute-start.10 = (bf16[128,512]{1,0:T(8,128)(2,1)S(1)}, bf16[128,512]{1,0:T(8,128)(2,1)S(1)}, u32[]{:S(2)}, u32[]{:S(2)}) collective-permute-start(bf16[128,512]{1,0:T(8,128)(2,1)S(1)} %get-tuple-element.14), channel_id=1, source_target_pairs={{32,0},{64,32},{96,64},{33,1},{65,33},{97,65},{34,2},{66,34},{98,6... | collective-permute-start | bytes 393224 | tf_op jit(solution)/shard_map/ppermute | solution.py:12
  80.8 10.0 %collective-permute-start.11 = (bf16[128,512]{1,0:T(8,128)(2,1)S(1)}, bf16[128,512]{1,0:T(8,128)(2,1)S(1)}, u32[]{:S(2)}, u32[]{:S(2)}) collective-permute-start(bf16[128,512]{1,0:T(8,128)(2,1)S(1)} %get-tuple-element.17), channel_id=1, source_target_pairs={{0,32},{32,64},{64,96},{1,33},{33,65},{65,97},{2,34},{34,66},{66,9... | collective-permute-start | bytes 393224 | tf_op jit(solution)/shard_map/ppermute | solution.py:12
  82.8 11.5 %collective-permute-start.12 = (bf16[128,512]{1,0:T(8,128)(2,1)S(1)}, bf16[128,512]{1,0:T(8,128)(2,1)S(1)}, u32[]{:S(2)}, u32[]{:S(2)}) collective-permute-start(bf16[128,512]{1,0:T(8,128)(2,1)S(1)} %get-tuple-element.16), channel_id=1, source_target_pairs={{1,0},{2,1},{3,2},{4,3},{5,4},{6,5},{7,6},{8,7},{9,8},{10,9},{11,1... | collective-permute-start | bytes 393224 | tf_op jit(solution)/shard_map/ppermute | solution.py:12
  84.1 10.2 %collective-permute-start.13 = (bf16[128,512]{1,0:T(8,128)(2,1)S(1)}, bf16[128,512]{1,0:T(8,128)(2,1)S(1)}, u32[]{:S(2)}, u32[]{:S(2)}) collective-permute-start(bf16[128,512]{1,0:T(8,128)(2,1)S(1)} %get-tuple-element.15), channel_id=1, source_target_pairs={{0,1},{1,2},{2,3},{3,4},{4,5},{5,6},{6,7},{7,8},{8,9},{9,10},{10,1... | collective-permute-start | bytes 393224 | tf_op jit(solution)/shard_map/ppermute | solution.py:12
  96.3 9.3 %collective-permute-start.14 = (bf16[256,512]{1,0:T(8,128)(2,1)S(1)}, bf16[256,512]{1,0:T(8,128)(2,1)S(1)}, u32[]{:S(2)}, u32[]{:S(2)}) collective-permute-start(bf16[256,512]{1,0:T(8,128)(2,1)S(1)} %get-tuple-element.34), channel_id=1, source_target_pairs={{128,0},{256,128},{384,256},{129,1},{257,129},{385,257},{130,2},{2... | collective-permute-start | bytes 786440 | tf_op jit(solution)/shard_map/ppermute | solution.py:12
  106.8 13.9 %collective-permute-start.15 = (bf16[128,512]{1,0:T(8,128)(2,1)S(1)}, bf16[128,512]{1,0:T(8,128)(2,1)S(1)}, u32[]{:S(2)}, u32[]{:S(2)}) collective-permute-start(bf16[128,512]{1,0:T(8,128)(2,1)S(1)} %get-tuple-element.10), channel_id=1, source_target_pairs={{32,0},{64,32},{96,64},{33,1},{65,33},{97,65},{34,2},{66,34},{98,6... | collective-permute-start | bytes 393224 | tf_op jit(solution)/shard_map/ppermute | solution.py:12
  110.0 10.7 %collective-permute-start.16 = (bf16[128,512]{1,0:T(8,128)(2,1)S(1)}, bf16[128,512]{1,0:T(8,128)(2,1)S(1)}, u32[]{:S(2)}, u32[]{:S(2)}) collective-permute-start(bf16[128,512]{1,0:T(8,128)(2,1)S(1)} %get-tuple-element.13), channel_id=1, source_target_pairs={{0,32},{32,64},{64,96},{1,33},{33,65},{65,97},{2,34},{34,66},{66,9... | collective-permute-start | bytes 393224 | tf_op jit(solution)/shard_map/ppermute | solution.py:12
  112.4 11.4 %collective-permute-start.17 = (bf16[128,512]{1,0:T(8,128)(2,1)S(1)}, bf16[128,512]{1,0:T(8,128)(2,1)S(1)}, u32[]{:S(2)}, u32[]{:S(2)}) collective-permute-start(bf16[128,512]{1,0:T(8,128)(2,1)S(1)} %get-tuple-element.12), channel_id=1, source_target_pairs={{1,0},{2,1},{3,2},{4,3},{5,4},{6,5},{7,6},{8,7},{9,8},{10,9},{11,1... | collective-permute-start | bytes 393224 | tf_op jit(solution)/shard_map/ppermute | solution.py:12
  113.7 10.1 %collective-permute-start.18 = (bf16[128,512]{1,0:T(8,128)(2,1)S(1)}, bf16[128,512]{1,0:T(8,128)(2,1)S(1)}, u32[]{:S(2)}, u32[]{:S(2)}) collective-permute-start(bf16[128,512]{1,0:T(8,128)(2,1)S(1)} %get-tuple-element.11), channel_id=1, source_target_pairs={{0,1},{1,2},{2,3},{3,4},{4,5},{5,6},{6,7},{7,8},{8,9},{9,10},{10,1... | collective-permute-start | bytes 393224 | tf_op jit(solution)/shard_map/ppermute | solution.py:12
  124.9 9.2 %collective-permute-start.19 = (bf16[256,512]{1,0:T(8,128)(2,1)S(1)}, bf16[256,512]{1,0:T(8,128)(2,1)S(1)}, u32[]{:S(2)}, u32[]{:S(2)}) collective-permute-start(bf16[256,512]{1,0:T(8,128)(2,1)S(1)} %get-tuple-element.36), channel_id=1, source_target_pairs={{128,0},{256,128},{384,256},{129,1},{257,129},{385,257},{130,2},{2... | collective-permute-start | bytes 786440 | tf_op jit(solution)/shard_map/ppermute | solution.py:12
  134.1 0.7 copy-start.12
  135.6 15.2 %collective-permute-start.20 = (bf16[128,512]{1,0:T(8,128)(2,1)S(1)}, bf16[128,512]{1,0:T(8,128)(2,1)S(1)}, u32[]{:S(2)}, u32[]{:S(2)}) collective-permute-start(bf16[128,512]{1,0:T(8,128)(2,1)S(1)} %get-tuple-element.6), channel_id=1, source_target_pairs={{32,0},{64,32},{96,64},{33,1},{65,33},{97,65},{34,2},{66,34},{98,6... | collective-permute-start | bytes 393224 | tf_op jit(solution)/shard_map/ppermute | solution.py:12
  138.9 11.9 %collective-permute-start.21 = (bf16[128,512]{1,0:T(8,128)(2,1)S(1)}, bf16[128,512]{1,0:T(8,128)(2,1)S(1)}, u32[]{:S(2)}, u32[]{:S(2)}) collective-permute-start(bf16[128,512]{1,0:T(8,128)(2,1)S(1)} %get-tuple-element.9), channel_id=1, source_target_pairs={{0,32},{32,64},{64,96},{1,33},{33,65},{65,97},{2,34},{34,66},{66,9... | collective-permute-start | bytes 393224 | tf_op jit(solution)/shard_map/ppermute | solution.py:12
  141.1 11.6 %collective-permute-start.22 = (bf16[128,512]{1,0:T(8,128)(2,1)S(1)}, bf16[128,512]{1,0:T(8,128)(2,1)S(1)}, u32[]{:S(2)}, u32[]{:S(2)}) collective-permute-start(bf16[128,512]{1,0:T(8,128)(2,1)S(1)} %get-tuple-element.8), channel_id=1, source_target_pairs={{1,0},{2,1},{3,2},{4,3},{5,4},{6,5},{7,6},{8,7},{9,8},{10,9},{11,1... | collective-permute-start | bytes 393224 | tf_op jit(solution)/shard_map/ppermute | solution.py:12
  142.4 10.3 %collective-permute-start.23 = (bf16[128,512]{1,0:T(8,128)(2,1)S(1)}, bf16[128,512]{1,0:T(8,128)(2,1)S(1)}, u32[]{:S(2)}, u32[]{:S(2)}) collective-permute-start(bf16[128,512]{1,0:T(8,128)(2,1)S(1)} %get-tuple-element.7), channel_id=1, source_target_pairs={{0,1},{1,2},{2,3},{3,4},{4,5},{5,6},{6,7},{7,8},{8,9},{9,10},{10,1... | collective-permute-start | bytes 393224 | tf_op jit(solution)/shard_map/ppermute | solution.py:12
  153.4 1.0 copy-start.13
  154.5 204.1 %copy-start.9 = (bf16[1,2,1,1,256,512]{5,4,1,3,2,0:T(8,128)(2,1)}, bf16[1,2,1,1,256,512]{5,4,1,3,2,0:T(8,128)(2,1)S(1)}, u32[]{:S(2)}) copy-start(bf16[1,2,1,1,256,512]{5,4,1,3,2,0:T(8,128)(2,1)S(1)} %bitcast_dynamic-update-slice_fusion) | copy-start | bytes 1572868
Sparse Core Ops, SparseCore 0:
  150.8 206.3 all-reduce.2
where the time goes:
time: 367 us; the launch traced here: 365 us
  waiting for transfers between devices  240 us (65%)
  starting transfers between devices  78 us (21%)
  matrix products  15.5 us (4%)
  between operations  15.5 us (4%)
  local copies, waits for them, and re-layouts  10.5 us (3%)
  other arithmetic  6.28 us (2%)
    unnamed x2, waiting for transfers between devices  203 us
    ppermute x24, starting transfers between devices, shifted(): lax.ppermute(value, axis, [(source, source + steps) for source in range(l...  78 us
    ppermute x24, waiting for transfers between devices, shifted(): lax.ppermute(value, axis, [(source, source + steps) for source in range(l...  37 us
  transfers between devices with their start and end apart: 25, of which 10 were waited for; matrix products, arithmetic and copies ran while one was open for 2% of the time, Pallas kernels for 0%

commit v1 on v0

v1 whole, which is shorter than its diff:
```python
import functools
import math

import jax
import jax.numpy as jnp
from jax import lax
from jax.experimental import pallas as pl
from jax.experimental.pallas import tpu as pltpu
from jax.sharding import PartitionSpec as P

MESH = pl.DeviceIdType.MESH
NT_DIMS = (((1,), (1,)), ((), ()))
TN_DIMS = (((0,), (0,)), ((), ()))
CHUNKS = 2
F32 = jnp.float32
BF16 = jnp.bfloat16


def slope_of(value):
    sigma = jax.nn.sigmoid(value)
    return sigma * (1.0 + value * (1.0 - sigma))


def kernel(
    scale, sections, rows, columns,
    stored, cotangent, weight, local_edges, halo_edges, pattern, pick,
    gw_out, gi_out,
    st_v, up_v, w_v, le_v, he_v, at_v, slope_v, dz_v, acc_v, hs_v, hr_v, res_v,
    gws_v, core_v, own_v, zs_v, zr_v, ys_v, yr_v,
    load_sem, out_sem, hs_sem, hr_sem, ps_sem, pr_sem, cs_sem, cr_sem, zs_sem, zr_sem, ys_sem, yr_sem,
):
    s = lax.axis_index("pipe")
    x = lax.axis_index("tx")
    y = lax.axis_index("ty")
    core = lax.rem(x, 2)
    y_lo = x // 2
    z = y // 4
    y_hi = lax.rem(y, 4)
    batches, nodes, width = up_v.shape[0], up_v.shape[2], w_v.shape[0]
    half = width // CHUNKS
    is_first = s == sections - 1

    sibling = {"tx": x + 1 - 2 * core}
    ring_z = [{"ty": lax.rem(y + 4 * k, columns)} for k in range(1, 8)]
    ring_y = [(a, b) for a in range(2) for b in range(4) if a or b]

    def y_device(a, b):
        return {"tx": lax.rem(x + 2 * a, rows), "ty": z * 4 + lax.rem(y_hi + b, 4)}

    send_to = [{"tx": x - 1}, {"tx": x + 1}, {"ty": y - 1}, {"ty": y + 1}]
    can_send = [x > 0, x < rows - 1, y > 0, y < columns - 1]
    can_recv = [x < rows - 1, x > 0, y < columns - 1, y > 0]

    loads = [
        pltpu.make_async_copy(weight, w_v, load_sem.at[0]),
        pltpu.make_async_copy(stored, st_v, load_sem.at[1]),
        pltpu.make_async_copy(local_edges, le_v, load_sem.at[2]),
        pltpu.make_async_copy(halo_edges, he_v, load_sem.at[3]),
    ]
    for copy in loads:
        copy.start()

    def up_load(m, k):
        return pltpu.make_async_copy(
            cotangent.at[m, :, pl.ds(k * half, half)], up_v.at[m, k], load_sem.at[4 + m * CHUNKS + k]
        )

    @pl.when(is_first)
    def _():
        for m in range(batches):
            for k in range(CHUNKS):
                up_load(m, k).start()

    barrier = pltpu.get_barrier_semaphore()

    def greet(device):
        pl.semaphore_signal(barrier, inc=1, device_id=device, device_id_type=MESH)

    for d in range(4):
        pl.when(can_send[d])(functools.partial(greet, send_to[d]))
    pl.when(s > 0)(lambda: greet({"pipe": s - 1}))
    pl.when(s < sections - 1)(lambda: greet({"pipe": s + 1}))
    for device in ring_z:
        greet(device)
    for a, b in ring_y:
        greet(y_device(a, b))

    for d in range(4):
        @pl.when(jnp.logical_not(can_recv[d]))
        def _():
            for m in range(batches):
                hr_v[m, d] = jnp.zeros(hr_v.shape[2:], BF16)

    def prepare_slope(m):
        value = jnp.dot(st_v[pl.ds(m * nodes, nodes), :], w_v[...], preferred_element_type=F32)
        slope_v[m] = slope_of(value)

    def prepare_edges(m):
        for b in range(2):
            for c in range(2):
                mask = pattern[m, b, c].astype(F32)
                block = (le_v[m, b, c].astype(F32) * mask).T
                at_v[m, pl.ds(c * 128, 128), pl.ds(b * 128, 128)] = block.astype(BF16)
            for d in range(4):
                mask = pattern[m, b, 2 + d].astype(F32)
                block = (he_v[m, d, b].astype(F32) * mask).T
                at_v[m, pl.ds(256 + d * 128, 128), pl.ds(b * 128, 128)] = block.astype(BF16)

    def halo_copy(m, d, k):
        return pltpu.make_async_remote_copy(
            hs_v.at[m, d, k], hr_v.at[m, d, k], hs_sem.at[m, d, k], hr_sem.at[m, d, k],
            device_id=send_to[d], device_id_type=MESH,
        )

    def pipe_copy(m, k):
        return pltpu.make_async_remote_copy(
            res_v.at[m, k], up_v.at[m, k], ps_sem.at[m, k], pr_sem.at[m, k],
            device_id={"pipe": s - 1}, device_id_type=MESH,
        )

    def out_copy(m, k):
        return pltpu.make_async_copy(
            res_v.at[m, k], gi_out.at[m, :, pl.ds(k * half, half)], out_sem.at[m, k]
        )

    def front(m):
        span = pl.ds(m * nodes, nodes)
        for k in range(CHUNKS):
            @pl.when(is_first)
            def _():
                up_load(m, k).wait()

            @pl.when(jnp.logical_not(is_first))
            def _():
                pipe_copy(m, k).wait_recv()

            cols = pl.ds(k * half, half)
            dz_v[span, cols] = (up_v[m, k].astype(F32) * slope_v[m, :, cols]).astype(BF16)
        for k in range(CHUNKS):
            dy = lax.dot_general(
                dz_v[span, :], w_v[pl.ds(k * half, half), :], NT_DIMS, preferred_element_type=F32
            ).astype(BF16)
            outward = jnp.dot(at_v[m, pl.ds(256, 512), :], dy, preferred_element_type=F32)
            for d in (2, 3, 0, 1):
                hs_v[m, d, k] = outward[d * 128 : (d + 1) * 128].astype(BF16)
                pl.when(can_send[d])(lambda: halo_copy(m, d, k).start())
            inner = jnp.dot(at_v[m, pl.ds(0, 256), :], dy, preferred_element_type=F32)
            acc_v[m, k] = up_v[m, k].astype(F32) + inner

    def back(m):
        for k in range(CHUNKS):
            for d in range(4):
                pl.when(can_recv[d])(lambda: halo_copy(m, d, k).wait_recv())
            lower = acc_v[m, k, pl.ds(0, 128), :]
            upper = acc_v[m, k, pl.ds(128, 128), :]
            for d in range(4):
                place = pick[m, d].astype(F32)
                arrived = hr_v[m, d, k].astype(F32)
                lower = lower + arrived * (1.0 - place)
                upper = upper + arrived * place
            res_v[m, k, pl.ds(0, 128), :] = lower.astype(BF16)
            res_v[m, k, pl.ds(128, 128), :] = upper.astype(BF16)
            pl.when(s > 0)(lambda: pipe_copy(m, k).start())
            out_copy(m, k).start()

    def core_copy():
        return pltpu.make_async_remote_copy(
            gws_v.at[1 - core], core_v, cs_sem, cr_sem, device_id=sibling, device_id_type=MESH
        )

    def weight_grad():
        for block in range(4):
            part = lax.dot_general(
                st_v[:, pl.ds(block * 128, 128)], dz_v[...], TN_DIMS, preferred_element_type=F32
            )
            gws_v[block % 2, block // 2] = part.astype(BF16)
            own_v[block % 2, block // 2] = part
        core_copy().start()

    def z_copy(k):
        to = lax.rem(z + k, 8)
        return pltpu.make_async_remote_copy(
            zs_v.at[to], zr_v.at[z], zs_sem.at[k], zr_sem.at[z],
            device_id=ring_z[k - 1], device_id_type=MESH,
        )

    def z_arrival(k):
        source = lax.rem(z + k, 8)
        return pltpu.make_async_remote_copy(
            zs_v.at[source], zr_v.at[source], zs_sem.at[k], zr_sem.at[source],
            device_id=ring_z[k - 1], device_id_type=MESH,
        )

    def weight_z():
        core_copy().wait_recv()
        for a in range(2):
            total = own_v[core, a] + core_v[a].astype(F32)
            for k in range(8):
                zs_v[k, a] = total[k * 16 : (k + 1) * 16].astype(BF16)
        for k in range(1, 8):
            z_copy(k).start()

    def y_copy(a, b):
        to_a, to_b = lax.rem(y_lo + a, 2), lax.rem(y_hi + b, 4)
        return pltpu.make_async_remote_copy(
            ys_v.at[to_a, to_b], yr_v.at[y_lo, y_hi], ys_sem.at[a, b], yr_sem.at[y_lo, y_hi],
            device_id=y_device(a, b), device_id_type=MESH,
        )

    def y_arrival(a, b):
        from_a, from_b = lax.rem(y_lo + a, 2), lax.rem(y_hi + b, 4)
        return pltpu.make_async_remote_copy(
            ys_v.at[from_a, from_b], yr_v.at[from_a, from_b], ys_sem.at[a, b], yr_sem.at[from_a, from_b],
            device_id=y_device(a, b), device_id_type=MESH,
        )

    def weight_y():
        for k in range(1, 8):
            z_arrival(k).wait_recv()
        for a in range(2):
            total = zs_v[z, a].astype(F32)
            for k in range(1, 8):
                total = total + zr_v[lax.rem(z + k, 8), a].astype(F32)
            for b in range(4):
                for q in range(4):
                    ys_v[a, b, pl.ds(q * 4, 4), :] = total[b * 4 : (b + 1) * 4, q * 128 : (q + 1) * 128]
        for a, b in ring_y:
            y_copy(a, b).start()

    def weight_out():
        total = ys_v[y_lo, y_hi]
        for a, b in ring_y:
            y_arrival(a, b).wait_recv()
            total = total + yr_v[lax.rem(y_lo + a, 2), lax.rem(y_hi + b, 4)]
        total = total * scale
        for q in range(4):
            gw_out[:, pl.ds(q * 128, 128)] = total[q * 4 : (q + 1) * 4]

    loads[0].wait()
    loads[1].wait()
    prepare_slope(0)
    loads[2].wait()
    loads[3].wait()
    prepare_edges(0)
    n_near = sum(c.astype(jnp.int32) for c in can_recv)
    n_pipe = (s > 0).astype(jnp.int32) + (s < sections - 1).astype(jnp.int32)
    pl.semaphore_wait(barrier, n_near + n_pipe + len(ring_z) + len(ring_y))

    front(0)
    prepare_slope(1)
    prepare_edges(1)
    front(1)
    weight_grad()
    weight_z()
    back(0)
    back(1)
    weight_y()
    weight_out()

    for m in range(batches):
        for k in range(CHUNKS):
            for d in range(4):
                pl.when(can_send[d])(lambda: halo_copy(m, d, k).wait_send())
            pl.when(s > 0)(lambda: pipe_copy(m, k).wait_send())
            out_copy(m, k).wait()
    core_copy().wait_send()
    for k in range(1, 8):
        z_copy(k).wait_send()
    for a, b in ring_y:
        y_copy(a, b).wait_send()


def per_device(mesh_shape, stored, cotangent, weight, local_edges, halo_edges, pattern, pick):
    sections, rows, columns = mesh_shape
    stashed = stored[0, :, 0, 0]
    batches, nodes, width = stashed.shape
    half = width // CHUNKS
    scale = 1.0 / math.sqrt(batches * nodes * rows * columns)
    hbm = pl.BlockSpec(memory_space=pl.ANY)
    smem = pl.BlockSpec(memory_space=pltpu.SMEM)
    dma = pltpu.SemaphoreType.DMA
    grad_weight, grad_input = pl.pallas_call(
        functools.partial(kernel, scale, sections, rows, columns),
        out_shape=(
            jax.ShapeDtypeStruct((4, width), F32),
            jax.ShapeDtypeStruct((batches, nodes, width), BF16),
        ),
        in_specs=[hbm] * 5 + [smem] * 2,
        out_specs=(pl.BlockSpec(memory_space=pltpu.VMEM), hbm),
        scratch_shapes=[
            pltpu.VMEM((batches * nodes, width), BF16),
            pltpu.VMEM((batches, CHUNKS, nodes, half), BF16),
            pltpu.VMEM((width, width), BF16),
            pltpu.VMEM((batches, 2, 2, 128, 128), BF16),
            pltpu.VMEM((batches, 4, 2, 128, 128), BF16),
            pltpu.VMEM((batches, 768, 256), BF16),
            pltpu.VMEM((batches, nodes, width), F32),
            pltpu.VMEM((batches * nodes, width), BF16),
            pltpu.VMEM((batches, CHUNKS, nodes, half), F32),
            pltpu.VMEM((batches, 4, CHUNKS, 128, half), BF16),
            pltpu.VMEM((batches, 4, CHUNKS, 128, half), BF16),
            pltpu.VMEM((batches, CHUNKS, nodes, half), BF16),
            pltpu.VMEM((2, 2, 128, width), BF16),
            pltpu.VMEM((2, 128, width), BF16),
            pltpu.VMEM((2, 2, 128, width), F32),
            pltpu.VMEM((8, 2, 16, width), BF16),
            pltpu.VMEM((8, 2, 16, width), BF16),
            pltpu.VMEM((2, 4, 16, 128), F32),
            pltpu.VMEM((2, 4, 16, 128), F32),
            dma((8,)),
            dma((batches, CHUNKS)),
            dma((batches, 4, CHUNKS)),
            dma((batches, 4, CHUNKS)),
            dma((batches, CHUNKS)),
            dma((batches, CHUNKS)),
            dma,
            dma,
            dma((8,)),
            dma((8,)),
            dma((2, 4)),
            dma((2, 4)),
        ],
        compiler_params=pltpu.CompilerParams(
            collective_id=0, has_side_effects=True, vmem_limit_bytes=48 << 20
        ),
        name="graph_backward",
    )(
        stashed.reshape(batches * nodes, width),
        cotangent[:, 0, 0],
        weight[0],
        local_edges[:, 0, 0],
        halo_edges[:, 0, 0],
        pattern[:, 0, 0],
        pick[:, 0, 0],
    )
    return grad_weight[None], grad_input[None, :, None, None]


def solution(mesh):
    shape = (mesh.shape["pipe"], mesh.shape["tx"], mesh.shape["ty"])
    in_specs = (
        P("pipe", None, "tx", "ty", None, None),
        P(None, "tx", "ty", None, None),
        P("pipe", None, None),
        P(None, "tx", "ty", None, None, None, None),
        P(None, "tx", "ty", None, None, None, None),
        P(None, "tx", "ty", None, None),
        P(None, "tx", "ty", None),
    )
    out_specs = (P("pipe", ("tx", "ty"), None), P("pipe", None, "tx", "ty", None, None))
    return jax.shard_map(
        functools.partial(per_device, shape),
        mesh=mesh,
        in_specs=in_specs,
        out_specs=out_specs,
        check_vma=False,
    )
```

time: 367 us -> 96.5 us (0.26)
  waiting for transfers between devices: 240 us -> 0 us
  Pallas kernels: 0 us -> 88.3 us
  starting transfers between devices: 78 us -> 0 us
  matrix products: 15.5 us -> 0 us
  between operations: 15.5 us -> 0.66 us
  other arithmetic: 6.28 us -> 0 us
    unnamed x2 -> x0, waiting for transfers between devices: 203 us -> none
    pallas_call x0 -> x1, Pallas kernels: none -> 88.3 us  [per_device(): pl.pallas_call(functools.partial(kernel, scale, sections, rows, columns),...]
    ppermute x24 -> x0, starting transfers between devices: 78 us -> none  [shifted(): lax.ppermute(value, axis, [(source, source + steps) for source in range(l...]
    ppermute x24 -> x0, waiting for transfers between devices: 37 us -> none  [shifted(): lax.ppermute(value, axis, [(source, source + steps) for source in range(l...]
    dot_general x30 -> x0, matrix products: 15.5 us -> none  [the longest x5 5.3 us: per_device(): jnp.dot(features, matrix, preferred_element_type=jnp.float32)]
  transfers between devices with their start and end apart: 25 -> 0, of which waited for: 10 -> 0; matrix products, arithmetic and copies ran while one was open for 2% -> 0% of each run, Pallas kernels for 0% -> 0%
where the time goes in v1:
time: 96.5 us; the launch traced here: 96.2 us
  Pallas kernels  88.3 us (92%)
  local copies, waits for them, and re-layouts  7.19 us (7%)
    pallas_call x1, Pallas kernels, per_device(): pl.pallas_call(functools.partial(kernel, scale, sections, rows, columns),...  88.3 us
    unnamed x16, local copies, waits for them, and re-layouts  7.19 us

profile of v1, /device:TPU:1, one launch (start us, length us, event | category | flops | bytes accessed | tf_op | source)
XLA Modules:
  0.0 96.2 jit_solution(16807754267780625637)
XLA Ops:
  0.6 0.0 copy-start.5
  0.6 0.0 copy-start.6
  0.7 0.7 copy-done.5
  1.3 0.0 copy-done.6
  1.3 0.0 copy-start
  1.3 1.0 %copy-done = bf16[1,2,1,1,256,512]{5,4,3,2,1,0:T(8,128)(2,1)S(1)} copy-done((bf16[1,2,1,1,256,512]{5,4,3,2,1,0:T(8,128)(2,1)S(1)}, bf16[1,2,1,1,256,512]{5,4,3,2,1,0:T(8,128)(2,1)}, u32[]{:S(2)}) %copy-start) | copy-done | bytes 524312
  2.4 0.0 copy-start.1
  2.4 1.0 %copy-done.1 = bf16[2,1,1,256,512]{4,3,2,1,0:T(8,128)(2,1)S(1)} copy-done((bf16[2,1,1,256,512]{4,3,2,1,0:T(8,128)(2,1)S(1)}, bf16[2,1,1,256,512]{4,3,2,1,0:T(8,128)(2,1)}, u32[]{:S(2)}) %copy-start.1) | copy-done | bytes 524312
  3.4 0.0 copy-start.2
  3.4 1.0 %copy-done.2 = bf16[1,512,512]{2,1,0:T(8,128)(2,1)S(1)} copy-done((bf16[1,512,512]{2,1,0:T(8,128)(2,1)S(1)}, bf16[1,512,512]{2,1,0:T(8,128)(2,1)}, u32[]{:S(2)}) %copy-start.2) | copy-done | bytes 524312
  4.5 0.0 copy-start.3
  4.5 1.0 %copy-done.3 = bf16[2,1,1,4,2,128,128]{6,5,4,3,2,1,0:T(8,128)(2,1)S(1)} copy-done((bf16[2,1,1,4,2,128,128]{6,5,4,3,2,1,0:T(8,128)(2,1)S(1)}, bf16[2,1,1,4,2,128,128]{6,5,4,3,2,1,0:T(8,128)(2,1)}, u32[]{:S(2)}) %copy-start.3) | copy-done | bytes 524312
  5.5 0.0 copy-start.4
  5.5 0.9 copy-done.4
  6.4 88.3 %graph_backward.1 = (f32[4,512]{1,0:T(4,128)S(1)}, bf16[2,256,512]{2,1,0:T(8,128)(2,1)S(1)}) custom-call(bf16[512,512]{1,0:T(8,128)(2,1)S(1)} %bitcast.11, bf16[2,256,512]{2,1,0:T(8,128)(2,1)S(1)} %bitcast.12, bf16[512,512]{1,0:T(8,128)(2,1)S(1)} %bitcast.13, bf16[2,2,2,128,128]{4,3,2,1,0:T(8,128)(2,1)S(1)} %bitcast.16, ...), custom_call_target="tpu_custom_call" | custom-call | tf_op jit(solution)/shard_map/graph_backward/pallas_call | solution.py:282
  94.8 0.6 copy.12
  95.4 0.8 copy.13
Async XLA Ops:
  0.6 0.7 copy-start.5
  0.6 0.7 copy-start.6
  1.3 1.0 %copy-start = (bf16[1,2,1,1,256,512]{5,4,3,2,1,0:T(8,128)(2,1)S(1)}, bf16[1,2,1,1,256,512]{5,4,3,2,1,0:T(8,128)(2,1)}, u32[]{:S(2)}) copy-start(bf16[1,2,1,1,256,512]{5,4,3,2,1,0:T(8,128)(2,1)} %param.7) | copy-start | bytes 1572868
  2.4 1.0 %copy-start.1 = (bf16[2,1,1,256,512]{4,3,2,1,0:T(8,128)(2,1)S(1)}, bf16[2,1,1,256,512]{4,3,2,1,0:T(8,128)(2,1)}, u32[]{:S(2)}) copy-start(bf16[2,1,1,256,512]{4,3,2,1,0:T(8,128)(2,1)} %param.8) | copy-start | bytes 1572868
  3.4 1.0 %copy-start.2 = (bf16[1,512,512]{2,1,0:T(8,128)(2,1)S(1)}, bf16[1,512,512]{2,1,0:T(8,128)(2,1)}, u32[]{:S(2)}) copy-start(bf16[1,512,512]{2,1,0:T(8,128)(2,1)} %param.9) | copy-start | bytes 1572868
  4.5 1.0 %copy-start.3 = (bf16[2,1,1,4,2,128,128]{6,5,4,3,2,1,0:T(8,128)(2,1)S(1)}, bf16[2,1,1,4,2,128,128]{6,5,4,3,2,1,0:T(8,128)(2,1)}, u32[]{:S(2)}) copy-start(bf16[2,1,1,4,2,128,128]{6,5,4,3,2,1,0:T(8,128)(2,1)} %param.11) | copy-start | bytes 1572868
  5.5 0.9 copy-start.4

commit v2 on v0

v2 whole, which is shorter than its diff:
```python
import functools
import math

import jax
import jax.numpy as jnp
from jax import lax
from jax.experimental import pallas as pl
from jax.experimental.pallas import tpu as pltpu
from jax.sharding import PartitionSpec as P

MESH = pl.DeviceIdType.MESH
NT_DIMS = (((1,), (1,)), ((), ()))
TN_DIMS = (((0,), (0,)), ((), ()))
CHUNKS = 2
F32 = jnp.float32
BF16 = jnp.bfloat16


def slope_of(value):
    sigma = jax.nn.sigmoid(value)
    return sigma * (1.0 + value * (1.0 - sigma))


def kernel(
    scale, rows, columns,
    stored, cotangent, weight, local_edges, halo_edges, pattern, pick,
    gw_out, gi_out,
    st3_v, cot3_v, w3_v, dz3_v, dy3_v,
    sec_st_v, sec_w_v, le_v, he_v, at_v, base_v, dyin_v, slope_v, dz_v, acc_v, hs_v, hr_v, res_v,
    own_v, gws_v, core_v, zs_v, zr_v, xs_v, xr_v, ys_v, yr_v,
    load_sem, own_sem, st_ss, st_rs, w_ss, w_rs, sib_ss, sib_rs, dy_ss, dy_rs, hs_sem, hr_sem,
    out_ss, out_rs, cs_sem, cr_sem, zs_sem, zr_sem, xs_sem, xr_sem, ys_sem, yr_sem, go_sem,
):
    p = lax.axis_index("pipe")
    x = lax.axis_index("tx")
    y = lax.axis_index("ty")
    core = lax.rem(x, 2)
    y_lo = x // 2
    z = y // 4
    y_hi = lax.rem(y, 4)
    nodes, width = 256, w3_v.shape[0]
    half = width // CHUNKS
    last = 3

    def host_plane(m, lo):
        return (1 - lo) * (3 - 2 * m) + lo * 2 * m

    def both(*conditions):
        return functools.reduce(jnp.logical_and, conditions)

    is_host = lax.rem(p + y_lo, 2) == 1
    mine = jnp.where(y_lo == 0, p == 1, p == 2).astype(jnp.int32)
    on_last = p == last

    sibling = {"tx": x + 1 - 2 * core}
    ring_z = [{"ty": lax.rem(y + 4 * k, columns)} for k in range(1, 8)]
    ring_y = [(a, b) for a in range(2) for b in range(4) if a or b]

    def y_device(a, b):
        return {"tx": lax.rem(x + 2 * a, rows), "ty": z * 4 + lax.rem(y_hi + b, 4)}

    def tile_row(row):
        return {"pipe": host_plane(mine, row // 2), "tx": row}

    send_to = [tile_row(x - 1), tile_row(x + 1), {"ty": y - 1}, {"ty": y + 1}]
    can_send = [x > 0, x < rows - 1, y > 0, y < columns - 1]
    can_recv = [x < rows - 1, x > 0, y < columns - 1, y > 0]

    def remote(src, dst, send_sem, recv_sem, device):
        return pltpu.make_async_remote_copy(
            src, dst, send_sem, recv_sem, device_id=device, device_id_type=MESH
        )

    def when(condition, action):
        pl.when(condition)(action)

    def cols(k):
        return pl.ds(k * half, half)

    last_loads = [
        lambda: pltpu.make_async_copy(stored, st3_v, load_sem.at[0]),
        lambda: pltpu.make_async_copy(weight, w3_v, load_sem.at[1]),
        lambda: pltpu.make_async_copy(cotangent, cot3_v, load_sem.at[2]),
    ]
    host_loads = [
        lambda: pltpu.make_async_copy(local_edges.at[mine], le_v, load_sem.at[3]),
        lambda: pltpu.make_async_copy(halo_edges.at[mine], he_v, load_sem.at[4]),
        lambda: pltpu.make_async_copy(cotangent.at[pl.ds(mine * nodes, nodes), :], base_v, load_sem.at[5]),
    ]

    def own_loads(section):
        return [
            pltpu.make_async_copy(
                stored.at[pl.ds(mine * nodes, nodes), :], sec_st_v.at[section], own_sem.at[0]
            ),
            pltpu.make_async_copy(weight, sec_w_v.at[section], own_sem.at[1]),
        ]

    @pl.when(on_last)
    def _():
        for load in last_loads:
            load().start()

    @pl.when(is_host)
    def _():
        for load in host_loads:
            load().start()

    for section in range(3):
        @pl.when(both(is_host, p == section))
        def _():
            for copy in own_loads(section):
                copy.start()

    barrier = pltpu.get_barrier_semaphore()

    def greet(device):
        pl.semaphore_signal(barrier, inc=1, device_id=device, device_id_type=MESH)

    for k in range(1, 4):
        greet({"pipe": lax.rem(p + k, 4)})
    greet(sibling)
    when(both(is_host, can_send[2]), lambda: greet(send_to[2]))
    when(both(is_host, can_send[3]), lambda: greet(send_to[3]))
    when(both(is_host, x == 1), lambda: greet(send_to[1]))
    when(both(is_host, x == 2), lambda: greet(send_to[0]))
    for device in ring_z:
        greet(device)
    for a, b in ring_y:
        greet(y_device(a, b))

    for d in range(4):
        @pl.when(both(is_host, jnp.logical_not(can_recv[d])))
        def _():
            for s in range(4):
                hr_v[s, d] = jnp.zeros(hr_v.shape[2:], BF16)

    def dy_copy(m, k):
        return remote(
            dy3_v.at[m, k], dyin_v.at[k], dy_ss.at[m, k], dy_rs.at[k], {"pipe": host_plane(m, y_lo)}
        )

    def dy_leaves(m):
        return host_plane(m, y_lo) != last

    def last_dz(m):
        span = pl.ds(m * nodes, nodes)
        value = jnp.dot(st3_v[span, :], w3_v[...], preferred_element_type=F32)
        dz3_v[span, :] = (cot3_v[span, :].astype(F32) * slope_of(value)).astype(BF16)

    def last_dy(m):
        span = pl.ds(m * nodes, nodes)
        for k in range(CHUNKS):
            dy3_v[m, k] = lax.dot_general(
                dz3_v[span, :], w3_v[cols(k), :], NT_DIMS, preferred_element_type=F32
            ).astype(BF16)

    def last_send(m):
        @pl.when(dy_leaves(m))
        def _():
            for k in range(CHUNKS):
                dy_copy(m, k).start()

        if m == 0:
            @pl.when(y_lo == 0)
            def _():
                dyin_v[...] = dy3_v[0]

    def w_rows(who):
        return pl.ds(who * (width // 2), width // 2)

    def section_sends(m):
        to = {"pipe": host_plane(m, y_lo)}
        return [
            remote(
                stored.at[pl.ds(m * nodes, nodes), :], sec_st_v.at[p], st_ss.at[m], st_rs.at[p], to
            ),
            remote(
                weight.at[w_rows(core), :], sec_w_v.at[p, w_rows(core), :], w_ss.at[m], w_rs.at[p], to
            ),
        ]

    def start_section_sends():
        for m in range(2):
            @pl.when(host_plane(m, y_lo) != p)
            def _():
                for copy in section_sends(m):
                    copy.start()

    def sibling_copy(section):
        part = sec_w_v.at[section, w_rows(core), :]
        return remote(part, part, sib_ss.at[section], sib_rs.at[section], sibling)

    def sibling_arrival(section):
        part = sec_w_v.at[section, w_rows(1 - core), :]
        return remote(part, part, sib_ss.at[section], sib_rs.at[section], sibling)

    def take_section(section):
        @pl.when(p == section)
        def _():
            for copy in own_loads(section):
                copy.wait()

        @pl.when(p != section)
        def _():
            part = sec_w_v.at[section, w_rows(core), :]
            remote(part, part, w_ss.at[0], w_rs.at[section], sibling).wait_recv()
            sibling_copy(section).start()
            whole = sec_st_v.at[section]
            remote(whole, whole, st_ss.at[0], st_rs.at[section], sibling).wait_recv()
            sibling_arrival(section).wait_recv()

        value = jnp.dot(sec_st_v[section], sec_w_v[section], preferred_element_type=F32)
        slope_v[...] = slope_of(value)

    def prepare_edges():
        for b in range(2):
            for d in range(4):
                mask = pattern[mine, b, 2 + d].astype(F32)
                block = (he_v[d, b].astype(F32) * mask).T
                at_v[pl.ds(256 + d * 128, 128), pl.ds(b * 128, 128)] = block.astype(BF16)
            for c in range(2):
                mask = pattern[mine, b, c].astype(F32)
                block = (le_v[b, c].astype(F32) * mask).T
                at_v[pl.ds(c * 128, 128), pl.ds(b * 128, 128)] = block.astype(BF16)

    def halo_copy(s, d, k):
        return remote(
            hs_v.at[s, d, k], hr_v.at[s, d, k], hs_sem.at[s, d, k], hr_sem.at[s, d, k], send_to[d]
        )

    def spread(s, k, dy, upstream):
        outward = jnp.dot(at_v[pl.ds(256, 512), :], dy, preferred_element_type=F32)
        for d in (2, 3, 0, 1):
            hs_v[s, d, k] = outward[d * 128 : (d + 1) * 128].astype(BF16)
            when(can_send[d], lambda: halo_copy(s, d, k).start())
        inner = jnp.dot(at_v[pl.ds(0, 256), :], dy, preferred_element_type=F32)
        acc_v[k] = upstream.astype(F32) + inner

    def front_last():
        for k in range(CHUNKS):
            @pl.when(jnp.logical_not(on_last))
            def _():
                dy_copy(0, k).wait_recv()

            spread(last, k, dyin_v[k], base_v[:, cols(k)])

    def front(s):
        for k in range(CHUNKS):
            dz_v[:, cols(k)] = (res_v[s + 1, k].astype(F32) * slope_v[:, cols(k)]).astype(BF16)
        for k in range(CHUNKS):
            dy = lax.dot_general(
                dz_v[...], sec_w_v[s, cols(k), :], NT_DIMS, preferred_element_type=F32
            ).astype(BF16)
            spread(s, k, dy, res_v[s + 1, k])

    def out_local(m, s, k):
        return pltpu.make_async_copy(res_v.at[s, k], gi_out.at[m, :, cols(k)], out_ss.at[s, k])

    def out_remote(m, s, k):
        return remote(
            res_v.at[s, k], gi_out.at[m, :, cols(k)], out_ss.at[s, k], out_rs.at[m, k], {"pipe": s}
        )

    def back(s):
        for k in range(CHUNKS):
            for d in range(4):
                when(can_recv[d], lambda: halo_copy(s, d, k).wait_recv())
            lower = acc_v[k, pl.ds(0, 128), :]
            upper = acc_v[k, pl.ds(128, 128), :]
            for d in range(4):
                place = pick[mine, d].astype(F32)
                arrived = hr_v[s, d, k].astype(F32)
                lower = lower + arrived * (1.0 - place)
                upper = upper + arrived * place
            res_v[s, k, pl.ds(0, 128), :] = lower.astype(BF16)
            res_v[s, k, pl.ds(128, 128), :] = upper.astype(BF16)
            when(p == s, lambda: out_local(mine, s, k).start())
            when(p != s, lambda: out_remote(mine, s, k).start())

    def core_copy(j):
        return remote(gws_v.at[j, 1 - core], core_v.at[j], cs_sem.at[j], cr_sem.at[j], sibling)

    def weight_grad(j, features, slopes):
        for block in range(4):
            part = lax.dot_general(
                features[:, pl.ds(block * 128, 128)], slopes[...], TN_DIMS, preferred_element_type=F32
            )
            gws_v[j, block % 2, block // 2] = part.astype(BF16)
            own_v[block % 2, block // 2] = part
        core_copy(j).start()

    def z_copy(j, k):
        to = lax.rem(z + k, 8)
        return remote(
            zs_v.at[j, to], zr_v.at[j, z], zs_sem.at[j, k], zr_sem.at[j, z], ring_z[k - 1]
        )

    def z_arrival(j, k):
        source = lax.rem(z + k, 8)
        return remote(
            zs_v.at[j, source], zr_v.at[j, source], zs_sem.at[j, k], zr_sem.at[j, source], ring_z[k - 1]
        )

    def weight_z(j):
        core_copy(j).wait_recv()
        for a in range(2):
            total = own_v[core, a] + core_v[j, a].astype(F32)
            for k in range(8):
                zs_v[j, k, a] = total[k * 16 : (k + 1) * 16].astype(BF16)
        for k in range(1, 8):
            z_copy(j, k).start()

    def z_totals(j):
        for k in range(1, 8):
            z_arrival(j, k).wait_recv()
        totals = []
        for a in range(2):
            total = zs_v[j, z, a].astype(F32)
            for k in range(1, 8):
                total = total + zr_v[j, lax.rem(z + k, 8), a].astype(F32)
            totals.append(total)
        return totals

    def x_copy(m, j):
        return remote(xs_v.at[j], xr_v.at[m], xs_sem.at[j], xr_sem.at[m], {"pipe": j})

    def weight_x(j):
        totals = z_totals(j)
        for a in range(2):
            xs_v[j, a] = totals[a].astype(BF16)
        when(p != j, lambda: x_copy(mine, j).start())

        @pl.when(p == j)
        def _():
            xr_v[mine] = xs_v[j]

    def y_copy(a, b):
        to_a, to_b = lax.rem(y_lo + a, 2), lax.rem(y_hi + b, 4)
        return remote(
            ys_v.at[to_a, to_b], yr_v.at[y_lo, y_hi], ys_sem.at[a, b], yr_sem.at[y_lo, y_hi], y_device(a, b)
        )

    def y_arrival(a, b):
        from_a, from_b = lax.rem(y_lo + a, 2), lax.rem(y_hi + b, 4)
        return remote(
            ys_v.at[from_a, from_b], yr_v.at[from_a, from_b], ys_sem.at[a, b],
            yr_sem.at[from_a, from_b], y_device(a, b),
        )

    def weight_y(totals):
        for a in range(2):
            for b in range(4):
                for q in range(4):
                    ys_v[a, b, pl.ds(q * 4, 4), :] = totals[a][
                        b * 4 : (b + 1) * 4, q * 128 : (q + 1) * 128
                    ]
        for a, b in ring_y:
            y_copy(a, b).start()

    def weight_out():
        total = ys_v[y_lo, y_hi]
        for a, b in ring_y:
            y_arrival(a, b).wait_recv()
            total = total + yr_v[lax.rem(y_lo + a, 2), lax.rem(y_hi + b, 4)]
        total = total * scale
        for q in range(4):
            gw_out[:, pl.ds(q * 128, 128)] = total[q * 4 : (q + 1) * 4]

    @pl.when(on_last)
    def _():
        last_loads[0]().wait()
        last_loads[1]().wait()
        last_loads[2]().wait()
        last_dz(1)
        last_dy(1)

    greeted = 18 + is_host.astype(jnp.int32) * (
        can_send[2].astype(jnp.int32)
        + can_send[3].astype(jnp.int32)
        + (x == 1).astype(jnp.int32)
        + (x == 2).astype(jnp.int32)
    )
    pl.semaphore_wait(barrier, greeted)

    @pl.when(both(p > 0, p < last))
    def _():
        start_section_sends()

    @pl.when(on_last)
    def _():
        last_send(1)
        last_dz(0)
        last_dy(0)
        last_send(0)

    @pl.when(is_host)
    def _():
        for load in host_loads:
            load().wait()
        prepare_edges()
        front_last()

        @pl.when(p != 0)
        def _():
            pl.semaphore_signal(go_sem, inc=1, device_id={"pipe": 0}, device_id_type=MESH)

    @pl.when(p == 0)
    def _():
        pl.semaphore_wait(go_sem, jnp.where(y_lo == 0, 2, 1))
        start_section_sends()

    @pl.when(on_last)
    def _():
        weight_grad(last, st3_v, dz3_v)

    @pl.when(is_host)
    def _():
        take_section(2)

    @pl.when(on_last)
    def _():
        weight_z(last)

    @pl.when(is_host)
    def _():
        back(last)
        for s in (2, 1, 0):
            front(s)
            weight_grad(s, sec_st_v.at[s], dz_v)
            if s > 0:
                take_section(s - 1)
            weight_z(s)
            if s < 2:
                weight_x(s + 1)
            back(s)
        weight_x(0)

    @pl.when(on_last)
    def _():
        weight_y(z_totals(last))

    @pl.when(p < last)
    def _():
        for m in range(2):
            @pl.when(host_plane(m, y_lo) != p)
            def _():
                x_copy(m, 0).wait_recv()
        weight_y([xr_v[0, a].astype(F32) + xr_v[1, a].astype(F32) for a in range(2)])

    weight_out()

    for m in range(2):
        @pl.when(host_plane(m, y_lo) != p)
        def _():
            for k in range(CHUNKS):
                out_remote(m, 0, k).wait_recv()

            @pl.when(p < last)
            def _():
                for copy in section_sends(m):
                    copy.wait_send()

        @pl.when(both(on_last, dy_leaves(m)))
        def _():
            for k in range(CHUNKS):
                dy_copy(m, k).wait_send()

    def sent_weights(j):
        core_copy(j).wait_send()
        for k in range(1, 8):
            z_copy(j, k).wait_send()

    @pl.when(is_host)
    def _():
        for s in range(4):
            for k in range(CHUNKS):
                for d in range(4):
                    when(can_send[d], lambda: halo_copy(s, d, k).wait_send())
                when(p == s, lambda: out_local(mine, s, k).wait())
                when(p != s, lambda: out_remote(mine, s, k).wait_send())
        for s in range(3):
            sent_weights(s)

            @pl.when(p != s)
            def _():
                sibling_copy(s).wait_send()
                x_copy(mine, s).wait_send()

    when(on_last, lambda: sent_weights(last))
    for a, b in ring_y:
        y_copy(a, b).wait_send()


def per_device(mesh_shape, stored, cotangent, weight, local_edges, halo_edges, pattern, pick):
    rows, columns = mesh_shape
    batches, nodes, width = stored.shape[1], stored.shape[4], stored.shape[5]
    half = width // CHUNKS
    scale = 1.0 / math.sqrt(batches * nodes * rows * columns)
    hbm = pl.BlockSpec(memory_space=pltpu.HBM)
    smem = pl.BlockSpec(memory_space=pltpu.SMEM)
    dma = pltpu.SemaphoreType.DMA
    vmem = pltpu.VMEM
    grad_weight, grad_input = pl.pallas_call(
        functools.partial(kernel, scale, rows, columns),
        out_shape=(
            jax.ShapeDtypeStruct((4, width), F32),
            jax.ShapeDtypeStruct((batches, nodes, width), BF16),
        ),
        in_specs=[hbm] * 5 + [smem] * 2,
        out_specs=(pl.BlockSpec(memory_space=pltpu.VMEM), hbm),
        scratch_shapes=[
            vmem((batches * nodes, width), BF16),
            vmem((batches * nodes, width), BF16),
            vmem((width, width), BF16),
            vmem((batches * nodes, width), BF16),
            vmem((batches, CHUNKS, nodes, half), BF16),
            vmem((3, nodes, width), BF16),
            vmem((3, width, width), BF16),
            vmem((2, 2, 128, 128), BF16),
            vmem((4, 2, 128, 128), BF16),
            vmem((768, 256), BF16),
            vmem((nodes, width), BF16),
            vmem((CHUNKS, nodes, half), BF16),
            vmem((nodes, width), F32),
            vmem((nodes, width), BF16),
            vmem((CHUNKS, nodes, half), F32),
            vmem((4, 4, CHUNKS, 128, half), BF16),
            vmem((4, 4, CHUNKS, 128, half), BF16),
            vmem((4, CHUNKS, nodes, half), BF16),
            vmem((2, 2, 128, width), F32),
            vmem((4, 2, 2, 128, width), BF16),
            vmem((4, 2, 128, width), BF16),
            vmem((4, 8, 2, 16, width), BF16),
            vmem((4, 8, 2, 16, width), BF16),
            vmem((3, 2, 16, width), BF16),
            vmem((2, 2, 16, width), BF16),
            vmem((2, 4, 16, 128), F32),
            vmem((2, 4, 16, 128), F32),
            dma((6,)),
            dma((2,)),
            dma((2,)),
            dma((3,)),
            dma((2,)),
            dma((3,)),
            dma((3,)),
            dma((3,)),
            dma((2, CHUNKS)),
            dma((CHUNKS,)),
            dma((4, 4, CHUNKS)),
            dma((4, 4, CHUNKS)),
            dma((4, CHUNKS)),
            dma((2, CHUNKS)),
            dma((4,)),
            dma((4,)),
            dma((4, 8)),
            dma((4, 8)),
            dma((3,)),
            dma((2,)),
            dma((2, 4)),
            dma((2, 4)),
            pltpu.SemaphoreType.REGULAR,
        ],
        compiler_params=pltpu.CompilerParams(
            collective_id=0, has_side_effects=True, vmem_limit_bytes=48 << 20
        ),
        name="graph_backward",
    )(
        stored.reshape(batches * nodes, width),
        cotangent.reshape(batches * nodes, width),
        weight[0],
        local_edges[:, 0, 0],
        halo_edges[:, 0, 0],
        pattern[:, 0, 0],
        pick[:, 0, 0],
    )
    return grad_weight[None], grad_input[None, :, None, None]


def solution(mesh):
    shape = (mesh.shape["tx"], mesh.shape["ty"])
    in_specs = (
        P("pipe", None, "tx", "ty", None, None),
        P(None, "tx", "ty", None, None),
        P("pipe", None, None),
        P(None, "tx", "ty", None, None, None, None),
        P(None, "tx", "ty", None, None, None, None),
        P(None, "tx", "ty", None, None),
        P(None, "tx", "ty", None),
    )
    out_specs = (P("pipe", ("tx", "ty"), None), P("pipe", None, "tx", "ty", None, None))
    return jax.shard_map(
        functools.partial(per_device, shape),
        mesh=mesh,
        in_specs=in_specs,
        out_specs=out_specs,
        check_vma=False,
    )
```

time: 367 us -> 88.2 us (0.24)
  waiting for transfers between devices: 240 us -> 0 us
  Pallas kernels: 0 us -> 80 us
  starting transfers between devices: 78 us -> 0 us
  matrix products: 15.5 us -> 0 us
  between operations: 15.5 us -> 0.66 us
  other arithmetic: 6.28 us -> 0 us
    unnamed x2 -> x0, waiting for transfers between devices: 203 us -> none
    pallas_call x0 -> x1, Pallas kernels: none -> 80 us  [per_device(): pl.pallas_call(functools.partial(kernel, scale, rows, columns), out_shape...]
    ppermute x24 -> x0, starting transfers between devices: 78 us -> none  [shifted(): lax.ppermute(value, axis, [(source, source + steps) for source in range(l...]
    ppermute x24 -> x0, waiting for transfers between devices: 37 us -> none  [shifted(): lax.ppermute(value, axis, [(source, source + steps) for source in range(l...]
    dot_general x30 -> x0, matrix products: 15.5 us -> none  [the longest x5 5.3 us: per_device(): jnp.dot(features, matrix, preferred_element_type=jnp.float32)]
  transfers between devices with their start and end apart: 25 -> 0, of which waited for: 10 -> 0; matrix products, arithmetic and copies ran while one was open for 2% -> 0% of each run, Pallas kernels for 0% -> 0%
where the time goes in v2:
time: 88.2 us; the launch traced here: 87.8 us
  Pallas kernels  80 us (91%)
  local copies, waits for them, and re-layouts  7.19 us (8%)
    pallas_call x1, Pallas kernels, per_device(): pl.pallas_call(functools.partial(kernel, scale, rows, columns), out_shape...  80 us
    unnamed x16, local copies, waits for them, and re-layouts  7.19 us

profile of v2, /device:TPU:1, one launch (start us, length us, event | category | flops | bytes accessed | tf_op | source)
XLA Modules:
  0.0 87.8 jit_solution(6184018327011126204)
XLA Ops:
  0.6 0.0 copy-start.5
  0.6 0.0 copy-start.6
  0.7 0.7 copy-done.5
  1.3 0.0 copy-done.6
  1.3 0.0 copy-start
  1.3 1.0 %copy-done = bf16[1,2,1,1,256,512]{5,4,3,2,1,0:T(8,128)(2,1)S(1)} copy-done((bf16[1,2,1,1,256,512]{5,4,3,2,1,0:T(8,128)(2,1)S(1)}, bf16[1,2,1,1,256,512]{5,4,3,2,1,0:T(8,128)(2,1)}, u32[]{:S(2)}) %copy-start) | copy-done | bytes 524312
  2.4 0.0 copy-start.1
  2.4 1.0 %copy-done.1 = bf16[2,1,1,256,512]{4,3,2,1,0:T(8,128)(2,1)S(1)} copy-done((bf16[2,1,1,256,512]{4,3,2,1,0:T(8,128)(2,1)S(1)}, bf16[2,1,1,256,512]{4,3,2,1,0:T(8,128)(2,1)}, u32[]{:S(2)}) %copy-start.1) | copy-done | bytes 524312
  3.4 0.0 copy-start.2
  3.4 1.0 %copy-done.2 = bf16[1,512,512]{2,1,0:T(8,128)(2,1)S(1)} copy-done((bf16[1,512,512]{2,1,0:T(8,128)(2,1)S(1)}, bf16[1,512,512]{2,1,0:T(8,128)(2,1)}, u32[]{:S(2)}) %copy-start.2) | copy-done | bytes 524312
  4.5 0.0 copy-start.3
  4.5 1.0 %copy-done.3 = bf16[2,1,1,4,2,128,128]{6,5,4,3,2,1,0:T(8,128)(2,1)S(1)} copy-done((bf16[2,1,1,4,2,128,128]{6,5,4,3,2,1,0:T(8,128)(2,1)S(1)}, bf16[2,1,1,4,2,128,128]{6,5,4,3,2,1,0:T(8,128)(2,1)}, u32[]{:S(2)}) %copy-start.3) | copy-done | bytes 524312
  5.5 0.0 copy-start.4
  5.5 0.9 %copy-done.4 = bf16[2,1,1,2,2,128,128]{6,5,4,3,2,1,0:T(8,128)(2,1)S(1)} copy-done((bf16[2,1,1,2,2,128,128]{6,5,4,3,2,1,0:T(8,128)(2,1)S(1)}, bf16[2,1,1,2,2,128,128]{6,5,4,3,2,1,0:T(8,128)(2,1)}, u32[]{:S(2)}) %copy-start.4) | copy-done | bytes 262168
  6.4 80.0 %graph_backward.1 = (f32[4,512]{1,0:T(4,128)S(1)}, bf16[2,256,512]{2,1,0:T(8,128)(2,1)S(1)}) custom-call(bf16[512,512]{1,0:T(8,128)(2,1)S(1)} %bitcast.11, bf16[512,512]{1,0:T(8,128)(2,1)S(1)} %bitcast.12, bf16[512,512]{1,0:T(8,128)(2,1)S(1)} %bitcast.13, bf16[2,2,2,128,128]{4,3,2,1,0:T(8,128)(2,1)S(1)} %bitcast.16, ...), custom_call_target="tpu_custom_call" | custom-call | tf_op jit(solution)/shard_map/graph_backward/pallas_call | solution.py:504
  86.4 0.6 copy.12
  87.0 0.8 copy.13
Async XLA Ops:
  0.6 0.7 copy-start.5
  0.6 0.7 copy-start.6
  1.3 1.0 %copy-start = (bf16[1,2,1,1,256,512]{5,4,3,2,1,0:T(8,128)(2,1)S(1)}, bf16[1,2,1,1,256,512]{5,4,3,2,1,0:T(8,128)(2,1)}, u32[]{:S(2)}) copy-start(bf16[1,2,1,1,256,512]{5,4,3,2,1,0:T(8,128)(2,1)} %param.7) | copy-start | bytes 1572868
  2.4 1.0 %copy-start.1 = (bf16[2,1,1,256,512]{4,3,2,1,0:T(8,128)(2,1)S(1)}, bf16[2,1,1,256,512]{4,3,2,1,0:T(8,128)(2,1)}, u32[]{:S(2)}) copy-start(bf16[2,1,1,256,512]{4,3,2,1,0:T(8,128)(2,1)} %param.8) | copy-start | bytes 1572868
  3.4 1.0 %copy-start.2 = (bf16[1,512,512]{2,1,0:T(8,128)(2,1)S(1)}, bf16[1,512,512]{2,1,0:T(8,128)(2,1)}, u32[]{:S(2)}) copy-start(bf16[1,512,512]{2,1,0:T(8,128)(2,1)} %param.9) | copy-start | bytes 1572868
  4.5 1.0 %copy-start.3 = (bf16[2,1,1,4,2,128,128]{6,5,4,3,2,1,0:T(8,128)(2,1)S(1)}, bf16[2,1,1,4,2,128,128]{6,5,4,3,2,1,0:T(8,128)(2,1)}, u32[]{:S(2)}) copy-start(bf16[2,1,1,4,2,128,128]{6,5,4,3,2,1,0:T(8,128)(2,1)} %param.11) | copy-start | bytes 1572868
  5.5 0.9 %copy-start.4 = (bf16[2,1,1,2,2,128,128]{6,5,4,3,2,1,0:T(8,128)(2,1)S(1)}, bf16[2,1,1,2,2,128,128]{6,5,4,3,2,1,0:T(8,128)(2,1)}, u32[]{:S(2)}) copy-start(bf16[2,1,1,2,2,128,128]{6,5,4,3,2,1,0:T(8,128)(2,1)} %param.10) | copy-start | bytes 786436

commit v3 on v2

--- a/solution.py
+++ b/solution.py
@@ -29,7 +29,7 @@
     sec_st_v, sec_w_v, le_v, he_v, at_v, base_v, dyin_v, slope_v, dz_v, acc_v, hs_v, hr_v, res_v,
     own_v, gws_v, core_v, zs_v, zr_v, xs_v, xr_v, ys_v, yr_v,
     load_sem, own_sem, st_ss, st_rs, w_ss, w_rs, sib_ss, sib_rs, dy_ss, dy_rs, hs_sem, hr_sem,
-    out_ss, out_rs, cs_sem, cr_sem, zs_sem, zr_sem, xs_sem, xr_sem, ys_sem, yr_sem, go_sem,
+    out_ss, out_rs, cs_sem, cr_sem, zs_sem, zr_sem, xs_sem, xr_sem, ys_sem, yr_sem,
 ):
     p = lax.axis_index("pipe")
     x = lax.axis_index("tx")
@@ -42,14 +42,14 @@
     half = width // CHUNKS
     last = 3
 
-    def host_plane(m, lo):
-        return (1 - lo) * (3 - 2 * m) + lo * 2 * m
+    def host_plane(m):
+        return 3 - 2 * m
 
     def both(*conditions):
         return functools.reduce(jnp.logical_and, conditions)
 
-    is_host = lax.rem(p + y_lo, 2) == 1
-    mine = jnp.where(y_lo == 0, p == 1, p == 2).astype(jnp.int32)
+    is_host = lax.rem(p, 2) == 1
+    mine = (p == 1).astype(jnp.int32)
     on_last = p == last
 
     sibling = {"tx": x + 1 - 2 * core}
@@ -60,7 +60,7 @@
         return {"tx": lax.rem(x + 2 * a, rows), "ty": z * 4 + lax.rem(y_hi + b, 4)}
 
     def tile_row(row):
-        return {"pipe": host_plane(mine, row // 2), "tx": row}
+        return {"tx": row}
 
     send_to = [tile_row(x - 1), tile_row(x + 1), {"ty": y - 1}, {"ty": y + 1}]
     can_send = [x > 0, x < rows - 1, y > 0, y < columns - 1]
@@ -137,11 +137,11 @@
 
     def dy_copy(m, k):
         return remote(
-            dy3_v.at[m, k], dyin_v.at[k], dy_ss.at[m, k], dy_rs.at[k], {"pipe": host_plane(m, y_lo)}
+            dy3_v.at[m, k], dyin_v.at[k], dy_ss.at[m, k], dy_rs.at[k], {"pipe": host_plane(m)}
         )
 
     def dy_leaves(m):
-        return host_plane(m, y_lo) != last
+        return host_plane(m) != last
 
     def last_dz(m):
         span = pl.ds(m * nodes, nodes)
@@ -161,16 +161,16 @@
             for k in range(CHUNKS):
                 dy_copy(m, k).start()
 
-        if m == 0:
-            @pl.when(y_lo == 0)
-            def _():
-                dyin_v[...] = dy3_v[0]
+    def last_keep():
+        @pl.when(host_plane(0) == last)
+        def _():
+            dyin_v[...] = dy3_v[0]
 
     def w_rows(who):
         return pl.ds(who * (width // 2), width // 2)
 
     def section_sends(m):
-        to = {"pipe": host_plane(m, y_lo)}
+        to = {"pipe": host_plane(m)}
         return [
             remote(
                 stored.at[pl.ds(m * nodes, nodes), :], sec_st_v.at[p], st_ss.at[m], st_rs.at[p], to
@@ -180,12 +180,11 @@
             ),
         ]
 
-    def start_section_sends():
-        for m in range(2):
-            @pl.when(host_plane(m, y_lo) != p)
-            def _():
-                for copy in section_sends(m):
-                    copy.start()
+    def start_section_sends(m):
+        @pl.when(host_plane(m) != p)
+        def _():
+            for copy in section_sends(m):
+                copy.start()
 
     def sibling_copy(section):
         part = sec_w_v.at[section, w_rows(core), :]
@@ -367,6 +366,7 @@
         for q in range(4):
             gw_out[:, pl.ds(q * 128, 128)] = total[q * 4 : (q + 1) * 4]
 
+
     @pl.when(on_last)
     def _():
         last_loads[0]().wait()
@@ -383,16 +383,18 @@
     )
     pl.semaphore_wait(barrier, greeted)
 
-    @pl.when(both(p > 0, p < last))
-    def _():
-        start_section_sends()
-
     @pl.when(on_last)
     def _():
         last_send(1)
         last_dz(0)
         last_dy(0)
         last_send(0)
+        last_keep()
+
+    @pl.when(p < last)
+    def _():
+        start_section_sends(0)
+        start_section_sends(1)
 
     @pl.when(is_host)
     def _():
@@ -401,14 +403,13 @@
         prepare_edges()
         front_last()
 
-        @pl.when(p != 0)
-        def _():
-            pl.semaphore_signal(go_sem, inc=1, device_id={"pipe": 0}, device_id_type=MESH)
-
-    @pl.when(p == 0)
-    def _():
-        pl.semaphore_wait(go_sem, jnp.where(y_lo == 0, 2, 1))
-        start_section_sends()
+    @pl.when(on_last)
+    def _():
+        for m in range(2):
+            @pl.when(dy_leaves(m))
+            def _():
+                for k in range(CHUNKS):
+                    dy_copy(m, k).wait_send()
 
     @pl.when(on_last)
     def _():
@@ -417,6 +418,7 @@
     @pl.when(is_host)
     def _():
         take_section(2)
+
 
     @pl.when(on_last)
     def _():
@@ -443,7 +445,7 @@
     @pl.when(p < last)
     def _():
         for m in range(2):
-            @pl.when(host_plane(m, y_lo) != p)
+            @pl.when(host_plane(m) != p)
             def _():
                 x_copy(m, 0).wait_recv()
         weight_y([xr_v[0, a].astype(F32) + xr_v[1, a].astype(F32) for a in range(2)])
@@ -451,7 +453,7 @@
     weight_out()
 
     for m in range(2):
-        @pl.when(host_plane(m, y_lo) != p)
+        @pl.when(host_plane(m) != p)
         def _():
             for k in range(CHUNKS):
                 out_remote(m, 0, k).wait_recv()
@@ -460,11 +462,6 @@
             def _():
                 for copy in section_sends(m):
                     copy.wait_send()
-
-        @pl.when(both(on_last, dy_leaves(m)))
-        def _():
-            for k in range(CHUNKS):
-                dy_copy(m, k).wait_send()
 
     def sent_weights(j):
         core_copy(j).wait_send()
@@ -559,10 +556,9 @@
             dma((2,)),
             dma((2, 4)),
             dma((2, 4)),
-            pltpu.SemaphoreType.REGULAR,
         ],
         compiler_params=pltpu.CompilerParams(
-            collective_id=0, has_side_effects=True, vmem_limit_bytes=48 << 20
+            collective_id=0, has_side_effects=True, vmem_limit_bytes=62 << 20
         ),
         name="graph_backward",
     )(

time: 88.2 us -> 80.3 us (0.910)
  local copies, waits for them, and re-layouts: 7.19 us -> 3.16 us
  Pallas kernels: 80 us -> 76.3 us
    unnamed x16 -> x2, local copies, waits for them, and re-layouts: 7.19 us -> 3.16 us
    pallas_call x1, Pallas kernels: 80 us -> 76.3 us  [per_device(): pl.pallas_call(functools.partial(kernel, scale, rows, columns), out_shape...]
where the time goes in v3:
time: 80.3 us; the launch traced here: 80.1 us
  Pallas kernels  76.3 us (95%)
  local copies, waits for them, and re-layouts  3.16 us (4%)
    pallas_call x1, Pallas kernels, per_device(): pl.pallas_call(functools.partial(kernel, scale, rows, columns), out_shape...  76.3 us
    unnamed x2, local copies, waits for them, and re-layouts  3.16 us

profile of v3, /device:TPU:1, one launch (start us, length us, event | category | flops | bytes accessed | tf_op | source)
XLA Modules:
  0.0 80.1 jit_solution(2564515881726636285)
XLA Ops:
  0.6 76.3 %graph_backward.1 = (f32[4,512]{1,0:T(4,128)}, bf16[2,256,512]{2,1,0:T(8,128)(2,1)}) custom-call(bf16[512,512]{1,0:T(8,128)(2,1)} %bitcast.11, bf16[512,512]{1,0:T(8,128)(2,1)} %bitcast.12, bf16[512,512]{1,0:T(8,128)(2,1)} %bitcast.13, bf16[2,2,2,128,128]{4,3,2,1,0:T(8,128)(2,1)} %bitcast.16, bf16[2,4,2,128,128]{4,3,2,1,0:T(8,128)(2,1)} %bitcast.14, ...), custom_call_target="tpu_custom_call" | custom-call | tf_op jit(solution)/shard_map/graph_backward/pallas_call | solution.py:501
  76.9 1.3 %copy.12 = f32[1,4,512]{2,1,0:T(4,128)} copy(f32[1,4,512]{2,1,0:T(4,128)} %bitcast.17) | data formatting | bytes 16384
  78.2 1.9 %copy.13 = bf16[1,2,1,1,256,512]{5,4,3,2,1,0:T(8,128)(2,1)} copy(bf16[1,2,1,1,256,512]{5,4,3,2,1,0:T(8,128)(2,1)} %bitcast.15) | data formatting | bytes 1048576

commit v4 on v3

--- a/solution.py
+++ b/solution.py
@@ -375,6 +375,12 @@
         last_dz(1)
         last_dy(1)
 
+    @pl.when(is_host)
+    def _():
+        for load in host_loads:
+            load().wait()
+        prepare_edges()
+
     greeted = 18 + is_host.astype(jnp.int32) * (
         can_send[2].astype(jnp.int32)
         + can_send[3].astype(jnp.int32)
@@ -398,9 +404,6 @@
 
     @pl.when(is_host)
     def _():
-        for load in host_loads:
-            load().wait()
-        prepare_edges()
         front_last()
 
     @pl.when(on_last)

time: 80.3 us -> 80.3 us (level)
  no operation moved by 1% of the time
where the time goes in v4:
time: 80.3 us; the launch traced here: 80 us
  Pallas kernels  76.2 us (95%)
  local copies, waits for them, and re-layouts  3.16 us (4%)
    pallas_call x1, Pallas kernels, per_device(): pl.pallas_call(functools.partial(kernel, scale, rows, columns), out_shape...  76.2 us
    unnamed x2, local copies, waits for them, and re-layouts  3.16 us

profile of v4, /device:TPU:1, one launch (start us, length us, event | category | flops | bytes accessed | tf_op | source)
XLA Modules:
  0.0 80.0 jit_solution(6251047236876978348)
XLA Ops:
  0.6 76.2 %graph_backward.1 = (f32[4,512]{1,0:T(4,128)}, bf16[2,256,512]{2,1,0:T(8,128)(2,1)}) custom-call(bf16[512,512]{1,0:T(8,128)(2,1)} %bitcast.11, bf16[512,512]{1,0:T(8,128)(2,1)} %bitcast.12, bf16[512,512]{1,0:T(8,128)(2,1)} %bitcast.13, bf16[2,2,2,128,128]{4,3,2,1,0:T(8,128)(2,1)} %bitcast.16, bf16[2,4,2,128,128]{4,3,2,1,0:T(8,128)(2,1)} %bitcast.14, ...), custom_call_target="tpu_custom_call" | custom-call | tf_op jit(solution)/shard_map/graph_backward/pallas_call | solution.py:504
  76.8 1.3 %copy.12 = f32[1,4,512]{2,1,0:T(4,128)} copy(f32[1,4,512]{2,1,0:T(4,128)} %bitcast.17) | data formatting | bytes 16384
  78.1 1.9 %copy.13 = bf16[1,2,1,1,256,512]{5,4,3,2,1,0:T(8,128)(2,1)} copy(bf16[1,2,1,1,256,512]{5,4,3,2,1,0:T(8,128)(2,1)} %bitcast.15) | data formatting | bytes 1048576
